TPU v7x, 32 devices: a whole 2x2x4 slice. The times are simulated.
32 devices in a mesh: row: 4 (over y, x), col: 8 (over z, core).
Axes of the slice: x: 2, y: 2, z: 4, core: 2. Of those that a mesh axis runs over, the one named last changes fastest.
Arguments:
- stiffness: float32 [12, 4, 128, 6144], P(None, 'row', None, 'col'), may hold values from -8 to 8
- lower_first: float32 [1024, 10, 4, 128], P('col', None, 'row'), may hold values from -0.1875 to 0.1875
- lower_second: float32 [1024, 8, 4, 128], P('col', None, 'row'), may hold values from -0.1875 to 0.1875
- diag_inv: float32 [2, 1024, 2, 4, 128], P(None, 'col', None, 'row'), as said below
Outputs:
- reduced: float32 [12, 4, 128, 6144], P(None, 'row', None, 'col')
Inputs may be any that keep to these rules, and one draw needn't show every extreme that they name: Each block of diag_inv, read as a 1024 x 1024 matrix, is zero above its diagonal and has a positive diagonal.
All inputs are finite; a program needn't handle non-finite values.
Results may differ from a plain program's by a relative error of at most 0.000086.
Values sent between devices are 32-bit elements; how exact they have to be, the bound alone decides.
A program may use at most 128 MiB of HBM per device.

v0:
```python
import jax
import jax.numpy as jnp
from jax import lax
from jax.sharding import PartitionSpec as P


def product(left, right):
    return jnp.dot(left, right, precision=lax.Precision.HIGH, preferred_element_type=jnp.float32)


def apply_cols(columns, factor):
    return lax.dot_general(
        columns,
        factor,
        (((0,), (0,)), ((), ())),
        precision=lax.Precision.HIGH,
        preferred_element_type=jnp.float32,
    )


def shards(stiffness, lower_first, lower_second, diag_inv):
    cycles = stiffness.shape[0]
    rblk = stiffness.shape[2]
    cdev = stiffness.shape[3]
    pcount = diag_inv.shape[2]
    nrow = lax.axis_size("row")
    nb = diag_inv.shape[1] * lax.axis_size("col")
    height = pcount * rblk
    matrix_rows = stiffness.reshape(cycles * rblk, cdev)
    inv_cols = lax.all_gather(diag_inv, "col", axis=1, tiled=True)
    inverse = inv_cols.reshape(2, nb, height)

    def own_rows(solved):
        grouped = solved.reshape(pcount, nrow, rblk, cdev)
        mine = lax.dynamic_slice_in_dim(grouped, lax.axis_index("row"), 1, 1)
        return mine.reshape(height, cdev)

    w_first = lax.psum(product(inverse[0], matrix_rows[:height]), "row")
    coupling = lax.all_gather(lower_first[:, :pcount], "col", axis=0, tiled=True).reshape(
        nb, height
    )
    w_second = lax.psum(
        product(inverse[1], matrix_rows[height : 2 * height] - apply_cols(coupling, w_first)), "row"
    )
    pieces = (
        lax.all_gather(lower_first[:, pcount:], "col", axis=0, tiled=True),
        lax.all_gather(lower_second, "col", axis=0, tiled=True),
    )
    count = pieces[0].shape[0]
    first_piece = pieces[0].reshape(count, -1)
    second_piece = pieces[1].reshape(count, -1)
    remain = (
        matrix_rows[2 * height :]
        - apply_cols(first_piece, w_first)
        - apply_cols(second_piece, w_second)
    )
    stacked = jnp.concatenate([own_rows(w_first), own_rows(w_second), remain], axis=0)
    return stacked.reshape(cycles, 1, rblk, cdev)


def solution(mesh):
    placed = (
        P(None, "row", None, "col"),
        P("col", None, "row", None),
        P("col", None, "row", None),
        P(None, "col", None, "row", None),
    )
    return jax.shard_map(
        shards, mesh=mesh, in_specs=placed, out_specs=P(None, "row", None, "col"), check_vma=False
    )
```

profile of v0, /device:TPU:0, one launch (start us, length us, event | category | flops | bytes accessed | tf_op | source)
XLA Modules:
  0.0 369.2 jit_solution(9611690720741950493)
XLA Ops:
  6.5 0.7 all-gather.5.cloned.1.call-update
  7.3 0.0 all-gather.7.cloned.1.call-start
  7.3 1.6 slice.37
  8.9 0.0 all-reduce.3.cloned.1.call-start
  8.9 1.5 fusion.16
  10.4 30.4 %all-gather.5.cloned.1.call-done = f32[2,1024,2,1,128]{4,3,2,1,0:T(1,128)} async-done(((f32[2,128,2,1,128]{4,3,2,1,0:T(1,128)}), f32[2,1024,2,1,128]{4,3,2,1,0:T(1,128)}) %all-gather.5.cloned.1.call-update) | async-done | bytes 2097168 | tf_op jit(solution)/shard_map/all_gather | solution.py:30
  40.8 7.8 %slice_reduce_fusion = (f32[1024,2,128]{2,1,0:T(2,128)S(1)}, f32[1024,2,128]{2,1,0:T(2,128)S(1)}) fusion(f32[2,1024,2,1,128]{4,3,2,1,0:T(1,128)} %all-gather.5.cloned.1.call-done), kind=kLoop, calls=%fused_computation.19 | loop fusion | bytes 4194304 | tf_op jit(solution)/shard_map/slice | solution.py:43
  48.7 3.1 fusion.13
  51.8 0.0 all-reduce.5.cloned.1.call-start
  51.9 0.3 copy.21
  52.2 12.0 %all-gather.7.cloned.1.call-done = f32[1024,2,1,128]{3,1,2,0:T(2,128)} async-done(((f32[128,2,1,128]{3,1,2,0:T(2,128)}), f32[1024,2,1,128]{3,1,2,0:T(2,128)}) %all-gather.7.cloned.1.call-update) | async-done | bytes 1048592 | tf_op jit(solution)/shard_map/all_gather | solution.py:39
  64.1 89.7 %all-reduce.3.cloned.1.call-done = f32[1024,768]{1,0:T(8,128)} async-done(((f32[1024,768]{1,0:T(8,128)}), f32[1024,768]{1,0:T(8,128)}) %all-reduce.3.cloned.1.call-update) | async-done | bytes 3145744 | tf_op jit(solution)/shard_map/psum | solution.py:38
  153.8 4.8 %fusion.8 = f32[256,768]{0,1:T(8,128)S(1)} fusion(f32[256,768]{0,1:T(8,128)S(1)} %copy.21, f32[1024,768]{1,0:T(8,128)} %all-reduce.3.cloned.1.call-done, f32[128,8,2,128]{3,2,1,0:T(2,128)} %bitcast.76), kind=kOutput, calls=%fused_computation.11 | convolution fusion | flops 1208156160 | bytes 5767168 | tf_op jit(solution)/shard_map/dot_general | solution.py:12
  158.6 3.1 convolution_bitcast_fusion
  161.7 0.0 all-gather.11.cloned.1.call-start
  161.8 0.5 all-gather.11.cloned.1.call-update
  162.3 0.2 all-gather.9.cloned.1.call-start
  162.6 0.8 slice.41
  163.4 3.8 %slice.39 = f32[8,1,128,768]{3,2,1,0:T(8,128)} slice(f32[12,1,128,768]{3,2,1,0:T(8,128)} %param.4), slice={[4:12], [0:1], [0:128], [0:768]} | slice | bytes 6291456 | tf_op jit(solution)/shard_map/slice | solution.py:53
  167.2 4.1 %copy.22 = f32[1024,768]{0,1:T(8,128)} copy(f32[1024,768]{1,0:T(8,128)} %bitcast.65) | data formatting | bytes 6291456 | tf_op jit(solution)/shard_map/slice | solution.py:53
  171.3 0.9 constant_dynamic-slice_fusion
  172.3 2.3 copy.20
  174.6 74.3 %all-reduce.5.cloned.1.call-done = f32[1024,768]{0,1:T(8,128)} async-done(((f32[1024,768]{0,1:T(8,128)}), f32[1024,768]{0,1:T(8,128)}) %all-reduce.5.cloned.1.call-update) | async-done | bytes 3145744 | tf_op jit(solution)/shard_map/psum | solution.py:42
  248.8 5.1 %reshape.36 = f32[2,4,128,768]{2,1,0,3:T(4,128)} reshape(f32[1024,768]{0,1:T(8,128)} %all-reduce.5.cloned.1.call-done) | data formatting | bytes 6291456 | tf_op jit(solution)/shard_map/reshape | solution.py:34
  254.0 4.6 %dynamic-slice_reduce_fusion = f32[2,128,768]{1,0,2:T(2,128)S(1)} fusion(f32[2,4,128,768]{2,1,0,3:T(4,128)} %reshape.36, s32[]{:T(128)S(6)} %select_n.4), kind=kLoop, calls=%fused_computation.22 | loop fusion | bytes 1572868 | tf_op jit(solution)/shard_map/dynamic_slice | solution.py:35
  258.5 0.9 copy.54
  259.5 37.7 %all-gather.11.cloned.1.call-done = f32[1024,8,1,128]{3,1,2,0:T(8,128)} async-done(((f32[128,8,1,128]{3,1,2,0:T(8,128)}), f32[1024,8,1,128]{3,1,2,0:T(8,128)}) %all-gather.11.cloned.1.call-update) | async-done | bytes 4194320 | tf_op jit(solution)/shard_map/all_gather | solution.py:47
  297.2 9.6 %fusion = f32[768,1024]{1,0:T(8,128)} fusion(f32[1024,768]{0,1:T(8,128)} %all-reduce.5.cloned.1.call-done, f32[128,8,8,128]{3,2,1,0:T(8,128)} %bitcast.66), kind=kOutput, calls=%fused_computation.1 | convolution fusion | flops 4831838208 | bytes 10485760 | tf_op jit(solution)/shard_map/dot_general | solution.py:12
  306.8 37.6 %all-gather.9.cloned.1.call-done = f32[1024,8,1,128]{3,1,2,0:T(8,128)} async-done(((f32[128,8,1,128]{3,1,2,0:T(8,128)}), f32[1024,8,1,128]{3,1,2,0:T(8,128)}) %all-gather.9.cloned.1.call-update) | async-done | bytes 4194320 | tf_op jit(solution)/shard_map/all_gather | solution.py:46
  344.3 9.4 %bitcast_subtract_fusion = f32[1024,768]{0,1:T(8,128)S(1)} fusion(f32[768,1024]{1,0:T(8,128)} %fusion, f32[1024,768]{0,1:T(8,128)} %copy.22, f32[1024,768]{1,0:T(8,128)S(1)} %copy-done, f32[128,8,8,128]{3,2,1,0:T(8,128)} %bitcast.69), kind=kOutput, calls=%fused_computation.7 | convolution fusion | flops 4833411072 | bytes 16777216 | tf_op jit(solution)/shard_map/dot_general | solution.py:12
  353.8 2.6 pad_maximum_fusion
  356.4 6.0 %copy.18 = f32[1536,768]{1,0:T(8,128)} copy(f32[1536,768]{0,1:T(8,128)} %pad_maximum_fusion) | data formatting | bytes 9437184 | tf_op jit(solution)/shard_map/concatenate | solution.py:57
  (13 shorter events, 0.1 us)
Async XLA Ops:
  6.5 34.3 %all-gather.5.cloned.1.call-start = ((), (), s32[]{:S(2)}) async-start(), calls=%async_computation | async-start | bytes 2359296 | tf_op jit(solution)/shard_map/all_gather | solution.py:30
  7.3 56.9 %all-gather.7.cloned.1.call-start = ((), (), s32[]{:S(2)}) async-start(), calls=%async_computation.2 | async-start | bytes 1179648 | tf_op jit(solution)/shard_map/all_gather | solution.py:39
  8.9 144.9 %all-reduce.3.cloned.1.call-start = ((), (), s32[]{:S(2)}) async-start(), calls=%async_computation.1 | async-start | bytes 6291456 | tf_op jit(solution)/shard_map/psum | solution.py:38
  51.8 197.0 %all-reduce.5.cloned.1.call-start = ((), (), s32[]{:S(2)}) async-start(), calls=%async_computation.3 | async-start | bytes 6291456 | tf_op jit(solution)/shard_map/psum | solution.py:42
  158.6 4.0 %copy-start.3 = (f32[128,10,1,128]{3,2,1,0:T(1,128)S(1)}, f32[128,10,1,128]{3,2,1,0:T(1,128)}, u32[]{:S(2)}) copy-start(f32[128,10,1,128]{3,2,1,0:T(1,128)} %param.5) | copy-start | bytes 1966084
  161.7 135.4 %all-gather.11.cloned.1.call-start = ((), (), s32[]{:S(2)}) async-start(), calls=%async_computation.5 | async-start | bytes 4718592 | tf_op jit(solution)/shard_map/all_gather | solution.py:47
  162.3 182.0 %all-gather.9.cloned.1.call-start = ((), (), s32[]{:S(2)}) async-start(), calls=%async_computation.4 | async-start | bytes 4718592 | tf_op jit(solution)/shard_map/all_gather | solution.py:46
  167.2 4.1 %copy-start = (f32[1024,768]{1,0:T(8,128)S(1)}, f32[1024,768]{1,0:T(8,128)}, u32[]{:S(2)}) copy-start(f32[1024,768]{1,0:T(8,128)} %all-reduce.3.cloned.1.call-done) | copy-start | bytes 9437188
  344.3 9.4 %copy-start.1 = (f32[256,768]{0,1:T(8,128)S(1)}, f32[256,768]{0,1:T(8,128)}, u32[]{:S(2)}) copy-start(f32[256,768]{0,1:T(8,128)} %copy.20) | copy-start | bytes 2359300
  344.3 9.4 %copy-start.2 = (f32[96,8,2,128]{3,1,2,0:T(8,128)S(1)}, f32[96,8,2,128]{3,1,2,0:T(8,128)}, u32[]{:S(2)}) copy-start(f32[96,8,2,128]{3,1,2,0:T(8,128)} %copy.54) | copy-start | bytes 2359300
Sparse Core Ops, SparseCore 0:
  8.9 31.8 all-gather.4
  42.4 21.6 all-gather.6
  67.2 86.5 all-reduce.2
  161.9 86.9 all-reduce.4
  250.3 46.8 all-gather.10
  298.6 45.6 all-gather.8
where the time goes:
time: 370 us; the launch traced here: 369 us
  waiting for transfers between devices  283 us (76%)
  local copies, waits for them, and re-layouts  39.8 us (11%)
  matrix products  30 us (8%)
  between operations  13.6 us (4%)
    psum x1, waiting for transfers between devices, shards(): w_first = lax.psum(product(inverse[0], matrix_rows[:height]), 'row')  89.7 us
    psum x1, waiting for transfers between devices, shards(): lax.psum(product(inverse[1], matrix_rows[height:2 * height] - apply_cols(...  74.3 us
    all_gather x1, waiting for transfers between devices, shards(): lax.all_gather(lower_second, 'col', axis=0, tiled=True)  37.7 us
    all_gather x1, waiting for transfers between devices, shards(): lax.all_gather(lower_first[:, pcount:], 'col', axis=0, tiled=True)  37.6 us
    all_gather x1, waiting for transfers between devices, shards(): inv_cols = lax.all_gather(diag_inv, 'col', axis=1, tiled=True)  30.4 us
    dot_general x3, matrix products, apply_cols(): lax.dot_general(columns, factor, (((0,), (0,)), ((), ())), precision=lax....  23.8 us
    all_gather x1, waiting for transfers between devices, shards(): lax.all_gather(lower_first[:, :pcount], 'col', axis=0, tiled=True)  12 us
    slice x2, local copies, waits for them, and re-layouts, shards(): matrix_rows[2 * height:] - apply_cols(first_piece, w_first)  7.89 us
  transfers between devices with their start and end apart: 6, of which 6 were waited for; matrix products, arithmetic and copies ran while one was open for 13% of the time, Pallas kernels for 0%

commit v1 on v0

--- a/solution.py
+++ b/solution.py
@@ -27,7 +27,12 @@
     nb = diag_inv.shape[1] * lax.axis_size("col")
     height = pcount * rblk
     matrix_rows = stiffness.reshape(cycles * rblk, cdev)
-    inv_cols = lax.all_gather(diag_inv, "col", axis=1, tiled=True)
+    ring = [diag_inv]
+    for hop in range(7):
+        ring.append(lax.ppermute(ring[-1], "col", [(dev, (dev + 1) % 8) for dev in range(8)]))
+    inv_cols = jnp.roll(
+        jnp.concatenate(ring[::-1], axis=1), (lax.axis_index("col") + 1) * ring[0].shape[1], axis=1
+    )
     inverse = inv_cols.reshape(2, nb, height)
 
     def own_rows(solved):

time: 370 us -> 295 us (0.80)
  waiting for transfers between devices: 283 us -> 211 us
  local copies, waits for them, and re-layouts: 39.8 us -> 35.6 us
    ppermute x0 -> x7, waiting for transfers between devices: none -> 50.9 us  [shards(): lax.ppermute(ring[-1], 'col', [(dev, (dev + 1) % 8) for dev in range(8)])]
    all_gather x1, waiting for transfers between devices: 37.7 us -> 0.01 us  [shards(): lax.all_gather(lower_second, 'col', axis=0, tiled=True)]
    all_gather x1, waiting for transfers between devices: 37.6 us -> 0.01 us  [shards(): lax.all_gather(lower_first[:, pcount:], 'col', axis=0, tiled=True)]
    all_gather x1 -> x0, waiting for transfers between devices: 30.4 us -> none  [shards(): inv_cols = lax.all_gather(diag_inv, 'col', axis=1, tiled=True)]
    all_gather x1, waiting for transfers between devices: 12 us -> 0.02 us  [shards(): lax.all_gather(lower_first[:, :pcount], 'col', axis=0, tiled=True)]
    reshape x1 -> x0, local copies, waits for them, and re-layouts: 5.13 us -> none  [own_rows(): grouped = solved.reshape(pcount, nrow, rblk, cdev)]
    psum x1, waiting for transfers between devices: 89.7 us -> 85.3 us  [shards(): w_first = lax.psum(product(inverse[0], matrix_rows[:height]), 'row')]
  transfers between devices with their start and end apart: 6 -> 12, of which waited for: 6 -> 9; matrix products, arithmetic and copies ran while one was open for 13% -> 14% of each run, Pallas kernels for 0% -> 0%
where the time goes in v1:
time: 295 us
  waiting for transfers between devices  211 us (72%)
  local copies, waits for them, and re-layouts  35.6 us (12%)
  matrix products  30.2 us (10%)
  between operations  14.8 us (5%)
    psum x1, waiting for transfers between devices, shards(): w_first = lax.psum(product(inverse[0], matrix_rows[:height]), 'row')  85.3 us
    psum x1, waiting for transfers between devices, shards(): lax.psum(product(inverse[1], matrix_rows[height:2 * height] - apply_cols(...  73.9 us
    ppermute x7, waiting for transfers between devices, shards(): lax.ppermute(ring[-1], 'col', [(dev, (dev + 1) % 8) for dev in range(8)])  50.9 us
    dot_general x3, matrix products, apply_cols(): lax.dot_general(columns, factor, (((0,), (0,)), ((), ())), precision=lax....  23.9 us
    slice x2, local copies, waits for them, and re-layouts, shards(): matrix_rows[2 * height:] - apply_cols(first_piece, w_first)  7.89 us
    slice x1, local copies, waits for them, and re-layouts, shards(): inverse[1]  6.61 us
    dot_general x2, matrix products, product(): jnp.dot(left, right, precision=lax.Precision.HIGH, preferred_element_type...  6.25 us
    concatenate x1, local copies, waits for them, and re-layouts, shards(): jnp.concatenate([own_rows(w_first), own_rows(w_second), remain], axis=0)  6.04 us
  transfers between devices with their start and end apart: 12, of which 9 were waited for; matrix products, arithmetic and copies ran while one was open for 14% of the time, Pallas kernels for 0%

profile of v1, /device:TPU:0, one launch (start us, length us, event | category | flops | bytes accessed | tf_op | source)
XLA Modules:
  0.0 294.9 jit_solution(480246162438617097)
XLA Ops:
  7.4 0.5 collective-permute-start
  7.9 8.4 %collective-permute-done = f32[2,128,2,1,128]{4,3,2,1,0:T(1,128)S(1)} collective-permute-done((f32[2,128,2,1,128]{4,3,2,1,0:T(1,128)}, f32[2,128,2,1,128]{4,3,2,1,0:T(1,128)S(1)}, u32[]{:S(2)}, u32[]{:S(2)}) %collective-permute-start) | collective-permute-done | bytes 262176 | tf_op jit(solution)/shard_map/ppermute | solution.py:32
  16.2 7.6 %collective-permute-done.1 = f32[2,128,2,1,128]{4,3,2,1,0:T(1,128)S(1)} collective-permute-done((f32[2,128,2,1,128]{4,3,2,1,0:T(1,128)S(1)}, f32[2,128,2,1,128]{4,3,2,1,0:T(1,128)S(1)}, u32[]{:S(2)}, u32[]{:S(2)}) %collective-permute-start.1) | collective-permute-done | bytes 262176 | tf_op jit(solution)/shard_map/ppermute | solution.py:32
  23.8 7.6 %collective-permute-done.2 = f32[2,128,2,1,128]{4,3,2,1,0:T(1,128)S(1)} collective-permute-done((f32[2,128,2,1,128]{4,3,2,1,0:T(1,128)S(1)}, f32[2,128,2,1,128]{4,3,2,1,0:T(1,128)S(1)}, u32[]{:S(2)}, u32[]{:S(2)}) %collective-permute-start.2) | collective-permute-done | bytes 262176 | tf_op jit(solution)/shard_map/ppermute | solution.py:32
  31.4 7.6 %collective-permute-done.3 = f32[2,128,2,1,128]{4,3,2,1,0:T(1,128)S(1)} collective-permute-done((f32[2,128,2,1,128]{4,3,2,1,0:T(1,128)S(1)}, f32[2,128,2,1,128]{4,3,2,1,0:T(1,128)S(1)}, u32[]{:S(2)}, u32[]{:S(2)}) %collective-permute-start.3) | collective-permute-done | bytes 262176 | tf_op jit(solution)/shard_map/ppermute | solution.py:32
  39.0 7.6 %collective-permute-done.4 = f32[2,128,2,1,128]{4,3,2,1,0:T(1,128)S(1)} collective-permute-done((f32[2,128,2,1,128]{4,3,2,1,0:T(1,128)S(1)}, f32[2,128,2,1,128]{4,3,2,1,0:T(1,128)S(1)}, u32[]{:S(2)}, u32[]{:S(2)}) %collective-permute-start.4) | collective-permute-done | bytes 262176 | tf_op jit(solution)/shard_map/ppermute | solution.py:32
  46.6 1.6 slice.38
  48.3 5.9 %collective-permute-done.5 = f32[2,128,2,1,128]{4,3,2,1,0:T(1,128)S(1)} collective-permute-done((f32[2,128,2,1,128]{4,3,2,1,0:T(1,128)S(1)}, f32[2,128,2,1,128]{4,3,2,1,0:T(1,128)S(1)}, u32[]{:S(2)}, u32[]{:S(2)}) %collective-permute-start.5) | collective-permute-done | bytes 262176 | tf_op jit(solution)/shard_map/ppermute | solution.py:32
  54.2 1.5 fusion.17
  55.7 6.3 %collective-permute-done.6 = f32[2,128,2,1,128]{4,3,2,1,0:T(1,128)S(1)} collective-permute-done((f32[2,128,2,1,128]{4,3,2,1,0:T(1,128)S(1)}, f32[2,128,2,1,128]{4,3,2,1,0:T(1,128)S(1)}, u32[]{:S(2)}, u32[]{:S(2)}) %collective-permute-start.6) | collective-permute-done | bytes 262176 | tf_op jit(solution)/shard_map/ppermute | solution.py:32
  62.2 0.2 constant_dynamic-update-slice_fusion.14
  63.6 0.2 constant_dynamic-update-slice_fusion.7
  65.3 6.6 %dynamic-slice_reduce_fusion = (f32[1024,2,128]{2,1,0:T(2,128)S(1)}, f32[1024,2,128]{2,1,0:T(2,128)S(1)}) fusion(f32[2,2048,2,1,128]{4,3,2,1,0:T(1,128)S(1)} %constant_dynamic-update-slice_fusion, s32[]{:T(128)S(6)} %add.29, s32[]{:T(128)S(6)} %select_n.18), kind=kLoop, calls=%fused_computation.19 | loop fusion | bytes 4194312 | tf_op jit(solution)/shard_map/slice | solution.py:48
  71.9 3.1 %fusion.14 = f32[1024,768]{1,0:T(8,128)} fusion(f32[256,768]{1,0:T(8,128)S(1)} %bitcast.61, f32[128,8,2,128]{3,2,1,0:T(2,128)S(1)} %bitcast.59), kind=kOutput, calls=%fused_computation.16 | convolution fusion | flops 1207959552 | bytes 4980736 | tf_op jit(solution)/shard_map/dot_general | solution.py:8
  75.0 0.2 all-reduce.5.cloned.1.call-start
  75.3 0.3 copy.24
  75.6 85.3 %all-reduce.3.cloned.1.call-done = f32[1024,768]{1,0:T(8,128)} async-done(((f32[1024,768]{1,0:T(8,128)}), f32[1024,768]{1,0:T(8,128)}) %all-reduce.3.cloned.1.call-update) | async-done | bytes 3145744 | tf_op jit(solution)/shard_map/psum | solution.py:43
  160.9 4.8 %fusion.8 = f32[256,768]{0,1:T(8,128)S(1)} fusion(f32[256,768]{0,1:T(8,128)S(1)} %copy.24, f32[1024,768]{1,0:T(8,128)} %all-reduce.3.cloned.1.call-done, f32[128,8,2,128]{3,2,1,0:T(2,128)} %bitcast.66), kind=kOutput, calls=%fused_computation.10 | convolution fusion | flops 1208156160 | bytes 5767168 | tf_op jit(solution)/shard_map/dot_general | solution.py:12
  165.7 3.1 %fusion.11 = f32[1024,768]{1,0:T(8,128)} fusion(f32[256,768]{0,1:T(8,128)S(1)} %fusion.8, f32[128,8,2,128]{3,2,1,0:T(2,128)S(1)} %bitcast.58), kind=kOutput, calls=%fused_computation.13 | convolution fusion | flops 1207959552 | bytes 4980736 | tf_op jit(solution)/shard_map/dot_general | solution.py:8
  168.9 0.7 all-gather.8.cloned.1.call-update
  169.7 0.8 slice.41
  170.5 3.8 %slice.39 = f32[8,1,128,768]{3,2,1,0:T(8,128)} slice(f32[12,1,128,768]{3,2,1,0:T(8,128)} %param.4), slice={[4:12], [0:1], [0:128], [0:768]} | slice | bytes 6291456 | tf_op jit(solution)/shard_map/slice | solution.py:58
  174.3 4.1 %copy.26 = f32[1024,768]{0,1:T(8,128)} copy(f32[1024,768]{1,0:T(8,128)} %bitcast.57) | data formatting | bytes 6291456 | tf_op jit(solution)/shard_map/slice | solution.py:58
  178.4 1.0 constant_dynamic-slice_fusion.1
  179.4 2.4 copy.23
  181.8 73.9 %all-reduce.5.cloned.1.call-done = f32[1024,768]{1,0:T(8,128)} async-done(((f32[1024,768]{1,0:T(8,128)}), f32[1024,768]{1,0:T(8,128)}) %all-reduce.5.cloned.1.call-update) | async-done | bytes 3145744 | tf_op jit(solution)/shard_map/psum | solution.py:47
  255.6 2.1 constant_dynamic-slice_fusion
  257.7 2.3 copy.25
  260.0 9.7 %fusion = f32[768,1024]{1,0:T(8,128)} fusion(f32[1024,768]{1,0:T(8,128)} %all-reduce.5.cloned.1.call-done, f32[128,8,8,128]{3,2,1,0:T(8,128)} %bitcast.70), kind=kOutput, calls=%fused_computation.1 | convolution fusion | flops 4831838208 | bytes 10485760 | tf_op jit(solution)/shard_map/dot_general | solution.py:12
  269.7 9.4 %bitcast_subtract_fusion = f32[1024,768]{0,1:T(8,128)S(1)} fusion(f32[768,1024]{1,0:T(8,128)} %fusion, f32[1024,768]{0,1:T(8,128)} %copy.26, f32[1024,768]{1,0:T(8,128)S(1)} %copy-done, f32[128,8,8,128]{3,2,1,0:T(8,128)} %bitcast.60), kind=kOutput, calls=%fused_computation.7 | convolution fusion | flops 4833411072 | bytes 16777216 | tf_op jit(solution)/shard_map/dot_general | solution.py:12
  279.2 2.6 pad_maximum_fusion
  281.8 6.0 %copy.21 = f32[1536,768]{1,0:T(8,128)} copy(f32[1536,768]{0,1:T(8,128)} %pad_maximum_fusion) | data formatting | bytes 9437184 | tf_op jit(solution)/shard_map/concatenate | solution.py:62
  (41 shorter events, 3.0 us)
Async XLA Ops:
  7.4 56.0 %copy-start.3 = (f32[2,128,2,1,128]{4,3,2,1,0:T(1,128)S(1)}, f32[2,128,2,1,128]{4,3,2,1,0:T(1,128)}, u32[]{:S(2)}) copy-start(f32[2,128,2,1,128]{4,3,2,1,0:T(1,128)} %param.7) | copy-start | bytes 786436
  7.4 68.2 %all-gather.4.cloned.1.call-start = ((), (), s32[]{:S(2)}) async-start(), calls=%async_computation.1 | async-start | bytes 1179648 | tf_op jit(solution)/shard_map/all_gather | solution.py:44
  7.4 8.8 %collective-permute-start = (f32[2,128,2,1,128]{4,3,2,1,0:T(1,128)}, f32[2,128,2,1,128]{4,3,2,1,0:T(1,128)S(1)}, u32[]{:S(2)}, u32[]{:S(2)}) collective-permute-start(f32[2,128,2,1,128]{4,3,2,1,0:T(1,128)} %param.7), channel_id=1, source_target_pairs={{0,1},{1,2},{2,3},{3,4},{4,5},{5,6},{6,7},{7,0},{8,9},{9,10},{10,1... | collective-permute-start | bytes 786440 | tf_op jit(solution)/shard_map/ppermute | solution.py:32
  16.2 7.6 %collective-permute-start.1 = (f32[2,128,2,1,128]{4,3,2,1,0:T(1,128)S(1)}, f32[2,128,2,1,128]{4,3,2,1,0:T(1,128)S(1)}, u32[]{:S(2)}, u32[]{:S(2)}) collective-permute-start(f32[2,128,2,1,128]{4,3,2,1,0:T(1,128)S(1)} %collective-permute-done), channel_id=1, source_target_pairs={{0,1},{1,2},{2,3},{3,4},{4,5},{5,6},{6,7},{7,0},{8,9},{9,10},{10,1... | collective-permute-start | bytes 786440 | tf_op jit(solution)/shard_map/ppermute | solution.py:32
  23.8 7.6 %collective-permute-start.2 = (f32[2,128,2,1,128]{4,3,2,1,0:T(1,128)S(1)}, f32[2,128,2,1,128]{4,3,2,1,0:T(1,128)S(1)}, u32[]{:S(2)}, u32[]{:S(2)}) collective-permute-start(f32[2,128,2,1,128]{4,3,2,1,0:T(1,128)S(1)} %collective-permute-done.1), channel_id=1, source_target_pairs={{0,1},{1,2},{2,3},{3,4},{4,5},{5,6},{6,7},{7,0},{8,9},{9,10},{10,1... | collective-permute-start | bytes 786440 | tf_op jit(solution)/shard_map/ppermute | solution.py:32
  31.4 7.6 %collective-permute-start.3 = (f32[2,128,2,1,128]{4,3,2,1,0:T(1,128)S(1)}, f32[2,128,2,1,128]{4,3,2,1,0:T(1,128)S(1)}, u32[]{:S(2)}, u32[]{:S(2)}) collective-permute-start(f32[2,128,2,1,128]{4,3,2,1,0:T(1,128)S(1)} %collective-permute-done.2), channel_id=1, source_target_pairs={{0,1},{1,2},{2,3},{3,4},{4,5},{5,6},{6,7},{7,0},{8,9},{9,10},{10,1... | collective-permute-start | bytes 786440 | tf_op jit(solution)/shard_map/ppermute | solution.py:32
  39.0 7.6 %collective-permute-start.4 = (f32[2,128,2,1,128]{4,3,2,1,0:T(1,128)S(1)}, f32[2,128,2,1,128]{4,3,2,1,0:T(1,128)S(1)}, u32[]{:S(2)}, u32[]{:S(2)}) collective-permute-start(f32[2,128,2,1,128]{4,3,2,1,0:T(1,128)S(1)} %collective-permute-done.3), channel_id=1, source_target_pairs={{0,1},{1,2},{2,3},{3,4},{4,5},{5,6},{6,7},{7,0},{8,9},{9,10},{10,1... | collective-permute-start | bytes 786440 | tf_op jit(solution)/shard_map/ppermute | solution.py:32
  46.6 7.6 %collective-permute-start.5 = (f32[2,128,2,1,128]{4,3,2,1,0:T(1,128)S(1)}, f32[2,128,2,1,128]{4,3,2,1,0:T(1,128)S(1)}, u32[]{:S(2)}, u32[]{:S(2)}) collective-permute-start(f32[2,128,2,1,128]{4,3,2,1,0:T(1,128)S(1)} %collective-permute-done.4), channel_id=1, source_target_pairs={{0,1},{1,2},{2,3},{3,4},{4,5},{5,6},{6,7},{7,0},{8,9},{9,10},{10,1... | collective-permute-start | bytes 786440 | tf_op jit(solution)/shard_map/ppermute | solution.py:32
  48.2 112.7 %all-reduce.3.cloned.1.call-start = ((), (), s32[]{:S(2)}) async-start(), calls=%async_computation | async-start | bytes 6291456 | tf_op jit(solution)/shard_map/psum | solution.py:43
  54.2 7.8 %collective-permute-start.6 = (f32[2,128,2,1,128]{4,3,2,1,0:T(1,128)S(1)}, f32[2,128,2,1,128]{4,3,2,1,0:T(1,128)S(1)}, u32[]{:S(2)}, u32[]{:S(2)}) collective-permute-start(f32[2,128,2,1,128]{4,3,2,1,0:T(1,128)S(1)} %collective-permute-done.5), channel_id=1, source_target_pairs={{0,1},{1,2},{2,3},{3,4},{4,5},{5,6},{6,7},{7,0},{8,9},{9,10},{10,1... | collective-permute-start | bytes 786440 | tf_op jit(solution)/shard_map/ppermute | solution.py:32
  75.0 180.6 %all-reduce.5.cloned.1.call-start = ((), (), s32[]{:S(2)}) async-start(), calls=%async_computation.2 | async-start | bytes 6291456 | tf_op jit(solution)/shard_map/psum | solution.py:47
  165.7 4.0 %copy-start.4 = (f32[128,10,1,128]{3,2,1,0:T(1,128)S(1)}, f32[128,10,1,128]{3,2,1,0:T(1,128)}, u32[]{:S(2)}) copy-start(f32[128,10,1,128]{3,2,1,0:T(1,128)} %param.5) | copy-start | bytes 1966084
  168.9 91.1 %all-gather.8.cloned.1.call-start = ((), (), s32[]{:S(2)}) async-start(), calls=%async_computation.4 | async-start | bytes 4718592 | tf_op jit(solution)/shard_map/all_gather | solution.py:52
  169.6 100.1 %all-gather.6.cloned.1.call-start = ((), (), s32[]{:S(2)}) async-start(), calls=%async_computation.3 | async-start | bytes 4718592 | tf_op jit(solution)/shard_map/all_gather | solution.py:51
  174.3 4.1 %copy-start = (f32[1024,768]{1,0:T(8,128)S(1)}, f32[1024,768]{1,0:T(8,128)}, u32[]{:S(2)}) copy-start(f32[1024,768]{1,0:T(8,128)} %all-reduce.3.cloned.1.call-done) | copy-start | bytes 9437188
  269.7 9.4 %copy-start.1 = (f32[256,768]{0,1:T(8,128)S(1)}, f32[256,768]{0,1:T(8,128)}, u32[]{:S(2)}) copy-start(f32[256,768]{0,1:T(8,128)} %copy.23) | copy-start | bytes 2359300
  269.7 9.4 %copy-start.2 = (f32[256,768]{0,1:T(8,128)S(1)}, f32[256,768]{0,1:T(8,128)}, u32[]{:S(2)}) copy-start(f32[256,768]{0,1:T(8,128)} %copy.25) | copy-start | bytes 2359300
Sparse Core Ops, SparseCore 0:
  48.3 24.7 all-gather.3
  171.3 46.8 all-gather.7
  219.8 45.6 all-gather.5
Sparse Core Ops, SparseCore 1:
  75.1 85.7 all-reduce.2
  168.9 86.6 all-reduce.4
